TPU v7x, 32 devices: a whole 2x2x4 slice. The times are simulated.
32 devices in a mesh: tile: 8 (over z, y), acq: 4 (over x, core).
Axes of the slice: x: 2, y: 2, z: 4, core: 2. Of those that a mesh axis runs over, the one named last changes fastest.
Arguments:
- phases: float32 [64, 131072], P('acq', 'tile'), may hold values from -6 to 6
- coherence: float32 [131072], P('tile'), may hold values from 0.1 to 1
- pixel_index: int32 [131072], P('tile'), may hold values from 0 to 8191
- send_list: int32 [64, 128], P('tile'), may hold values from 0 to 16383, as said below
- counts: int32 [8, 8], P('tile'), may hold values from 16 to 128, as said below
- band_width: int32 [64], replicated, may hold values from 1 to 8
Outputs:
- residual: float32 [64, 8192], P('acq', 'tile')
- screen: float32 [64, 64, 1024], P('acq', 'tile')
Inputs may be any that keep to these rules, and one draw needn't show every extreme that they name: `counts`: for every device two owner tiles (the same for all devices, possibly one) receive all 128 slots; the others receive between 16 and 63. `send_list`: the live entries of one device's rows are distinct local scatterer indices; entries beyond a row's count are valid indices that carry no data.
All inputs are finite; a program needn't handle non-finite values.
Results may differ from a plain program's by a relative error of at most 0.0003.
Values sent between devices are 32-bit elements; how exact they have to be, the bound alone decides.
No kernel may reach another device: no remote copies, remote signals or barrier semaphores. Data moves between devices by JAX's collectives and lax.ppermute only.
A program may use at most 64 MiB of HBM per device.

v0:
```python
import jax
import jax.numpy as jnp
from jax import lax
from jax.sharding import PartitionSpec as P

ACQ = 64
ROWS_DEV = 8
COLS = 1024
RADIUS = 4
SLAB_PIX = 8192
min_weight = 0.1


def with_halo(cells, sides, width):
    for axis, dim in sides:
        count = lax.axis_size(axis)
        ends = count - 1
        head = lax.slice_in_dim(cells, 0, width, axis=dim)
        tail = lax.slice_in_dim(cells, cells.shape[dim] - width, cells.shape[dim], axis=dim)
        cells = jnp.concatenate(
            [
                lax.ppermute(tail, axis, [(i, (i + 1) % count) for i in range(ends)]),
                cells,
                lax.ppermute(head, axis, [((i + 1) % count, i) for i in range(ends)]),
            ],
            axis=dim,
        )
    return cells


def temporal_matrix(band_width):
    positions = jnp.arange(ACQ, dtype=jnp.int32)
    lower = jnp.maximum(positions - band_width, 0)
    upper = jnp.minimum(positions + band_width, ACQ - 1)
    inside = (positions[None, :] >= lower[:, None]) & (positions[None, :] <= upper[:, None])
    window = (upper - lower + 1).astype(jnp.float32)
    return jnp.eye(ACQ, dtype=jnp.float32) - inside.astype(jnp.float32) / window[:, None]


def kernel_weights():
    return [
        (RADIUS + 1 - abs(offset - RADIUS)) / float((RADIUS + 1) ** 2)
        for offset in range(2 * RADIUS + 1)
    ]


def smooth(padded_rows):
    weights = kernel_weights()
    row_count = padded_rows.shape[-2] - 2 * RADIUS
    vertical = weights[0] * padded_rows[..., 0:row_count, :]
    for offset in range(1, 2 * RADIUS + 1):
        vertical = vertical + weights[offset] * padded_rows[..., offset : offset + row_count, :]
    column_count = vertical.shape[-1]
    pad_width = [(0, 0)] * (vertical.ndim - 1) + [(RADIUS, RADIUS)]
    widened = jnp.pad(vertical, pad_width)
    total = weights[0] * widened[..., 0:column_count]
    for offset in range(1, 2 * RADIUS + 1):
        total = total + weights[offset] * widened[..., offset : offset + column_count]
    return total


def apply_highpass(highpass, series):
    return jnp.dot(
        highpass, series, precision=lax.Precision.HIGHEST, preferred_element_type=jnp.float32
    )


def shards(phases, coherence, pixel_index, send_list, counts, band_width):
    acq_loc = phases.shape[0]
    capacity = send_list.shape[1]
    highpass = temporal_matrix(band_width)
    live_slot = jnp.arange(capacity, dtype=jnp.int32)[None, :] < counts[0][:, None]
    slot_weight = jnp.where(live_slot, coherence[send_list], jnp.float32(0.0))
    slot_pixel = pixel_index[send_list]
    outgoing = phases[:, send_list] * slot_weight[None]
    arrived, arrived_weight, arrived_pixel = (
        lax.all_to_all(outgoing, "tile", split_axis=1, concat_axis=1, tiled=True),
        lax.all_to_all(slot_weight[None], "tile", split_axis=1, concat_axis=1, tiled=True),
        lax.all_to_all(slot_pixel[None], "tile", split_axis=1, concat_axis=1, tiled=True),
    )
    targets = arrived_pixel.reshape(-1)
    phase_image = (
        jnp.zeros((acq_loc, SLAB_PIX), jnp.float32).at[:, targets].add(arrived.reshape(acq_loc, -1))
    )
    weight_sum = jnp.zeros((SLAB_PIX,), jnp.float32).at[targets].add(arrived_weight.reshape(-1))
    series = lax.all_to_all(phase_image, "acq", split_axis=1, concat_axis=0, tiled=True)
    phase_image = lax.all_to_all(
        apply_highpass(highpass, series), "acq", split_axis=0, concat_axis=1, tiled=True
    )
    stacked = jnp.concatenate([phase_image, weight_sum[None, :]], axis=0).reshape(
        acq_loc + 1, ROWS_DEV, COLS
    )
    padded = with_halo(stacked, (("tile", 1),), RADIUS)
    smoothed = smooth(padded)
    screen = smoothed[:acq_loc] / jnp.maximum(smoothed[acq_loc], min_weight)
    flattened = screen.reshape(acq_loc, SLAB_PIX)
    sampled = flattened[:, arrived_pixel[0]]
    returned = lax.all_to_all(sampled, "tile", split_axis=1, concat_axis=1, tiled=True)
    residual = jnp.where(live_slot[None], phases[:, send_list] - returned, jnp.float32(0.0))
    return (residual.reshape(acq_loc, -1), screen)


def solution(mesh):
    return jax.shard_map(
        shards,
        mesh=mesh,
        in_specs=(P("acq", "tile"), P("tile"), P("tile"), P("tile", None), P("tile", None), P()),
        out_specs=(P("acq", "tile"), P("acq", "tile", None)),
        check_vma=False,
    )
```

profile of v0, /device:TPU:0, one launch (start us, length us, event | category | flops | bytes accessed | tf_op | source)
XLA Modules:
  0.0 134.2 jit_solution(15241608124049495737)
XLA Ops:
  0.6 0.0 copy-start
  0.6 0.0 copy-start.1
  0.7 0.7 fusion.58
  1.4 0.1 copy-done
  1.5 0.0 copy-start.3
  1.5 10.5 %gather_fusion.1 = s32[1024]{0:T(1024)} fusion(s32[16384]{0:T(1024)S(1)} %copy-done, s32[1024]{0:T(1024)S(1)} %fusion.58), kind=kCustom, calls=%fused_computation.1 | custom fusion | bytes 12288 | tf_op jit(solution)/shard_map/gather | solution.py:74
  12.0 7.3 %all-to-all-start = ((s32[1,8,128]{2,0,1:T(1,128)}), s32[1,8,128]{2,0,1:T(1,128)S(1)}, u32[]{:S(2)}, u32[]{:S(2)}) async-start(s32[1,8,128]{2,0,1:T(1,128)} %bitcast.5), calls=%async_computation | async-start | bytes 8192 | tf_op jit(solution)/shard_map/all_to_all | solution.py:79
  19.3 0.0 copy-done.1
  19.3 6.2 %gather_fusion.2 = f32[1024]{0:T(1024)S(1)} fusion(f32[16384]{0:T(1024)S(1)} %copy-done.1, s32[1024]{0:T(1024)S(1)} %fusion.58), kind=kCustom, calls=%fused_computation.2 | custom fusion | bytes 12288 | tf_op jit(solution)/shard_map/gather | solution.py:73
  25.5 0.0 copy-done.3
  25.5 0.0 copy-start.4
  25.5 4.6 %copy.23 = f32[16,16384]{0,1:T(8,128)} copy(f32[16,16384]{1,0:T(8,128)S(1)} %copy-done.3) | data formatting | bytes 2097152 | tf_op args[0]
  30.1 6.2 %gather_fusion = f32[1024,16]{1,0:T(8,128)S(1)} fusion(f32[16,16384]{0,1:T(8,128)} %copy.23, s32[1024]{0:T(1024)S(1)} %fusion.58), kind=kCustom, calls=%fused_computation | custom fusion | bytes 135168 | tf_op jit(solution)/shard_map/gather | solution.py:99
  36.3 0.2 copy.24
  36.4 0.0 copy-done.4
  36.5 0.1 bitcast_select_fusion
  36.5 0.7 bitcast_multiply_fusion
  37.2 0.0 all-to-all-done
  37.2 6.0 %all-to-all-start.1 = ((f32[16,8,128]{2,0,1:T(8,128)}), f32[16,8,128]{2,0,1:T(8,128)S(1)}, u32[]{:S(2)}, u32[]{:S(2)}) async-start(f32[16,8,128]{2,0,1:T(8,128)} %bitcast_multiply_fusion), calls=%async_computation.1 | async-start | bytes 131072 | tf_op jit(solution)/shard_map/all_to_all | solution.py:77
  43.2 6.9 %all-to-all-done.1 = f32[16,8,128]{2,0,1:T(8,128)S(1)} async-done(((f32[16,8,128]{2,0,1:T(8,128)}), f32[16,8,128]{2,0,1:T(8,128)S(1)}, u32[]{:S(2)}, u32[]{:S(2)}) %all-to-all-start.1) | async-done | bytes 65568 | tf_op jit(solution)/shard_map/all_to_all | solution.py:77
  50.1 0.2 copy.26
  50.3 0.0 copy-start.5
  50.3 8.2 %scatter_custom_fusion = f32[16,8192]{0,1:T(8,128)} fusion(s32[1024]{0:T(1024)S(1)} %bitcast.63, f32[1024,16]{1,0:T(8,128)S(1)} %copy.26, f32[]{:T(128)} %constant.2.clone.1), kind=kCustom, calls=%fused_computation.6 | custom fusion | flops 16384 | bytes 524292 | tf_op jit(solution)/shard_map/scatter-add | solution.py:83
  58.5 3.5 %copy.27 = f32[16,4,2048]{2,0,1:T(8,128)} copy(f32[16,4,2048]{0,2,1:T(8,128)} %bitcast.55) | data formatting | bytes 1048576 | tf_op jit(solution)/shard_map/all_to_all | solution.py:86
  62.0 3.5 %all-to-all-start.2 = ((f32[16,4,2048]{2,0,1:T(8,128)}), f32[16,4,2048]{2,0,1:T(8,128)S(1)}, u32[]{:S(2)}, u32[]{:S(2)}) async-start(f32[16,4,2048]{2,0,1:T(8,128)} %copy.27), calls=%async_computation.2 | async-start | bytes 1048576 | tf_op jit(solution)/shard_map/all_to_all | solution.py:86
  65.5 0.0 copy-done.5
  65.5 0.1 div.34
  65.6 0.1 ge.32
  65.7 0.1 le.27
  65.8 0.7 compare_select_fusion.1
  66.4 7.9 %all-to-all-done.2 = f32[16,4,2048]{2,0,1:T(8,128)S(1)} async-done(((f32[16,4,2048]{2,0,1:T(8,128)}), f32[16,4,2048]{2,0,1:T(8,128)S(1)}, u32[]{:S(2)}, u32[]{:S(2)}) %all-to-all-start.2) | async-done | bytes 524320 | tf_op jit(solution)/shard_map/all_to_all | solution.py:86
  74.3 3.3 %all-to-all-start.4 = ((f32[1,8,128]{2,0,1:T(1,128)}), f32[1,8,128]{2,0,1:T(1,128)S(1)}, u32[]{:S(2)}, u32[]{:S(2)}) async-start(f32[1,8,128]{2,0,1:T(1,128)} %compare_select_fusion.1), calls=%async_computation.4 | async-start | bytes 8192 | tf_op jit(solution)/shard_map/all_to_all | solution.py:78
  77.6 1.4 %fusion.43 = f32[4,16,2048]{2,1,0:T(8,128)} fusion(f32[64,2048,1]{1,0,2:T(8,128)S(1)} %bitcast.57, f32[4,16]{1,0:T(4,128)S(1)} %div.34, s32[4,16]{1,0:T(4,128)S(1)} %le.27, s32[4,16]{1,0:T(4,128)S(1)} %ge.32, s32[4,16]{1,0:T(4,128)S(1)} %multiply_add_fusion), kind=kOutput, calls=%fused_computation.77 | convolution fusion | flops 100696064 | bytes 1049600 | tf_op jit(solution)/shard_map/dot_general | solution.py:63
  79.0 4.9 %all-to-all-done.4 = f32[1,8,128]{2,0,1:T(1,128)S(1)} async-done(((f32[1,8,128]{2,0,1:T(1,128)}), f32[1,8,128]{2,0,1:T(1,128)S(1)}, u32[]{:S(2)}, u32[]{:S(2)}) %all-to-all-start.4) | async-done | bytes 4128 | tf_op jit(solution)/shard_map/all_to_all | solution.py:78
  83.9 3.5 %all-to-all-start.3 = ((f32[4,16,2048]{2,1,0:T(8,128)}), f32[4,16,2048]{2,1,0:T(8,128)S(1)}, u32[]{:S(2)}, u32[]{:S(2)}) async-start(f32[4,16,2048]{2,1,0:T(8,128)} %fusion.43), calls=%async_computation.3 | async-start | bytes 1048576 | tf_op jit(solution)/shard_map/all_to_all | solution.py:87
  87.4 5.9 %scatter_custom_fusion.1 = f32[8192]{0:T(1024)S(1)} fusion(s32[1024]{0:T(1024)S(1)} %bitcast.64, f32[1024]{0:T(1024)S(1)} %bitcast.65, f32[]{:T(128)} %constant.2.clone.1), kind=kCustom, calls=%fused_computation.88 | custom fusion | flops 1024 | bytes 32772 | tf_op jit(solution)/shard_map/scatter-add | solution.py:85
  93.4 2.8 %all-to-all-done.3 = f32[4,16,2048]{2,1,0:T(8,128)S(1)} async-done(((f32[4,16,2048]{2,1,0:T(8,128)}), f32[4,16,2048]{2,1,0:T(8,128)S(1)}, u32[]{:S(2)}, u32[]{:S(2)}) %all-to-all-start.3) | async-done | bytes 524320 | tf_op jit(solution)/shard_map/all_to_all | solution.py:87
  96.2 0.3 copy.28
  96.6 0.2 concatenate.21
  96.8 0.1 fusion.61
  97.0 2.5 %collective-permute-start = (f32[17,4,1024]{2,1,0:T(4,128)S(1)}, f32[17,4,1024]{2,1,0:T(4,128)S(1)}, u32[]{:S(2)}, u32[]{:S(2)}) collective-permute-start(f32[17,4,1024]{2,1,0:T(4,128)S(1)} %get-tuple-element.2), channel_id=1, source_target_pairs={{0,4},{4,8},{8,12},{12,16},{16,20},{20,24},{24,28},{1,5},{5,9},{9,... | collective-permute-start | bytes 835592 | tf_op jit(solution)/shard_map/ppermute | solution.py:22
  99.5 1.3 collective-permute-start.1
  100.8 10.3 %collective-permute-done = f32[17,4,1024]{2,1,0:T(4,128)S(1)} collective-permute-done((f32[17,4,1024]{2,1,0:T(4,128)S(1)}, f32[17,4,1024]{2,1,0:T(4,128)S(1)}, u32[]{:S(2)}, u32[]{:S(2)}) %collective-permute-start) | collective-permute-done | bytes 278560 | tf_op jit(solution)/shard_map/ppermute | solution.py:22
  111.1 0.0 collective-permute-done.1
  111.1 1.0 fusion.21
  112.1 1.2 fusion.10
  113.4 0.1 slice_divide_fusion
  113.5 0.0 copy-start.2
  113.5 2.7 %copy.29 = f32[16,8,1024]{0,2,1:T(8,128)} copy(f32[16,8,1024]{2,1,0:T(8,128)S(1)} %slice_divide_fusion) | data formatting | bytes 1048576 | tf_op jit(solution)/shard_map/div | solution.py:95
  116.2 5.0 %gather_fusion.3 = f32[1024,16]{1,0:T(8,128)S(1)} fusion(f32[16,8192]{0,1:T(8,128)} %bitcast.56, s32[1024]{0:T(1024)S(1)} %fusion.60), kind=kCustom, calls=%fused_computation.3 | custom fusion | bytes 135168 | tf_op jit(solution)/shard_map/gather | solution.py:97
  121.2 0.8 copy.30
  122.0 4.7 %all-to-all-start.5 = ((f32[16,8,128]{2,0,1:T(8,128)}), f32[16,8,128]{2,0,1:T(8,128)S(1)}, u32[]{:S(2)}, u32[]{:S(2)}) async-start(f32[16,8,128]{2,0,1:T(8,128)} %bitcast.22), calls=%async_computation.5 | async-start | bytes 131072 | tf_op jit(solution)/shard_map/all_to_all | solution.py:98
  126.6 0.1 iota_compare_fusion.5
  126.7 6.8 %all-to-all-done.5 = f32[16,8,128]{2,0,1:T(8,128)S(1)} async-done(((f32[16,8,128]{2,0,1:T(8,128)}), f32[16,8,128]{2,0,1:T(8,128)S(1)}, u32[]{:S(2)}, u32[]{:S(2)}) %all-to-all-start.5) | async-done | bytes 65568 | tf_op jit(solution)/shard_map/all_to_all | solution.py:98
  133.5 0.6 copy_bitcast_fusion
  134.2 0.0 copy-done.2
  (9 shorter events, 0.1 us)
Async XLA Ops:
  0.6 0.8 copy-start
  0.6 18.7 %copy-start.1 = (f32[16384]{0:T(1024)S(1)}, f32[16384]{0:T(1024)}, u32[]{:S(2)}) copy-start(f32[16384]{0:T(1024)} %param.7) | copy-start | bytes 196612
  1.5 24.0 %copy-start.3 = (f32[16,16384]{1,0:T(8,128)S(1)}, f32[16,16384]{1,0:T(8,128)}, u32[]{:S(2)}) copy-start(f32[16,16384]{1,0:T(8,128)} %param.6) | copy-start | bytes 3145732
  12.0 25.2 %all-to-all-start = ((s32[1,8,128]{2,0,1:T(1,128)}), s32[1,8,128]{2,0,1:T(1,128)S(1)}, u32[]{:S(2)}, u32[]{:S(2)}) async-start(s32[1,8,128]{2,0,1:T(1,128)} %bitcast.5), calls=%async_computation | async-start | bytes 8192 | tf_op jit(solution)/shard_map/all_to_all | solution.py:79
  25.5 11.0 %copy-start.4 = (s32[1,8]{1,0:T(1,128)S(1)}, s32[1,8]{1,0:T(1,128)}, u32[]{:S(2)}) copy-start(s32[1,8]{1,0:T(1,128)} %param.10) | copy-start | bytes 100
  37.2 12.9 %all-to-all-start.1 = ((f32[16,8,128]{2,0,1:T(8,128)}), f32[16,8,128]{2,0,1:T(8,128)S(1)}, u32[]{:S(2)}, u32[]{:S(2)}) async-start(f32[16,8,128]{2,0,1:T(8,128)} %bitcast_multiply_fusion), calls=%async_computation.1 | async-start | bytes 131072 | tf_op jit(solution)/shard_map/all_to_all | solution.py:77
  50.3 15.2 %copy-start.5 = (s32[64]{0:T(128)S(1)}, s32[64]{0:T(128)}, u32[]{:S(2)}) copy-start(s32[64]{0:T(128)} %param.11) | copy-start | bytes 772
  62.0 12.3 %all-to-all-start.2 = ((f32[16,4,2048]{2,0,1:T(8,128)}), f32[16,4,2048]{2,0,1:T(8,128)S(1)}, u32[]{:S(2)}, u32[]{:S(2)}) async-start(f32[16,4,2048]{2,0,1:T(8,128)} %copy.27), calls=%async_computation.2 | async-start | bytes 1048576 | tf_op jit(solution)/shard_map/all_to_all | solution.py:86
  74.3 9.6 %all-to-all-start.4 = ((f32[1,8,128]{2,0,1:T(1,128)}), f32[1,8,128]{2,0,1:T(1,128)S(1)}, u32[]{:S(2)}, u32[]{:S(2)}) async-start(f32[1,8,128]{2,0,1:T(1,128)} %compare_select_fusion.1), calls=%async_computation.4 | async-start | bytes 8192 | tf_op jit(solution)/shard_map/all_to_all | solution.py:78
  83.9 12.3 %all-to-all-start.3 = ((f32[4,16,2048]{2,1,0:T(8,128)}), f32[4,16,2048]{2,1,0:T(8,128)S(1)}, u32[]{:S(2)}, u32[]{:S(2)}) async-start(f32[4,16,2048]{2,1,0:T(8,128)} %fusion.43), calls=%async_computation.3 | async-start | bytes 1048576 | tf_op jit(solution)/shard_map/all_to_all | solution.py:87
  97.0 14.1 %collective-permute-start = (f32[17,4,1024]{2,1,0:T(4,128)S(1)}, f32[17,4,1024]{2,1,0:T(4,128)S(1)}, u32[]{:S(2)}, u32[]{:S(2)}) collective-permute-start(f32[17,4,1024]{2,1,0:T(4,128)S(1)} %get-tuple-element.2), channel_id=1, source_target_pairs={{0,4},{4,8},{8,12},{12,16},{16,20},{20,24},{24,28},{1,5},{5,9},{9,... | collective-permute-start | bytes 835592 | tf_op jit(solution)/shard_map/ppermute | solution.py:22
  99.5 11.7 %collective-permute-start.1 = (f32[17,4,1024]{2,1,0:T(4,128)S(1)}, f32[17,4,1024]{2,1,0:T(4,128)S(1)}, u32[]{:S(2)}, u32[]{:S(2)}) collective-permute-start(f32[17,4,1024]{2,1,0:T(4,128)S(1)} %get-tuple-element.3), channel_id=1, source_target_pairs={{4,0},{8,4},{12,8},{16,12},{20,16},{24,20},{28,24},{5,1},{9,5},{13... | collective-permute-start | bytes 835592 | tf_op jit(solution)/shard_map/ppermute | solution.py:24
  113.5 20.7 %copy-start.2 = (f32[16,8,1024]{2,1,0:T(8,128)}, f32[16,8,1024]{2,1,0:T(8,128)S(1)}, u32[]{:S(2)}) copy-start(f32[16,8,1024]{2,1,0:T(8,128)S(1)} %slice_divide_fusion) | copy-start | bytes 1572868
  122.0 11.6 %all-to-all-start.5 = ((f32[16,8,128]{2,0,1:T(8,128)}), f32[16,8,128]{2,0,1:T(8,128)S(1)}, u32[]{:S(2)}, u32[]{:S(2)}) async-start(f32[16,8,128]{2,0,1:T(8,128)} %bitcast.22), calls=%async_computation.5 | async-start | bytes 131072 | tf_op jit(solution)/shard_map/all_to_all | solution.py:98
where the time goes:
time: 135 us; the launch traced here: 134 us
  local copies, waits for them, and re-layouts  40.9 us (30%)
  waiting for transfers between devices  39.7 us (29%)
  starting transfers between devices  31.9 us (24%)
  other arithmetic  19.3 us (14%)
  matrix products  1.42 us (1%)
    gather x1, local copies, waits for them, and re-layouts, shards(): slot_pixel = pixel_index[send_list]  10.5 us
    ppermute x1, waiting for transfers between devices, with_halo(): lax.ppermute(tail, axis, [(i, (i + 1) % count) for i in range(ends)])  10.3 us
    scatter-add x1, other arithmetic, shards(): jnp.zeros((acq_loc, SLAB_PIX), jnp.float32).at[:, targets]  8.21 us
    all_to_all x1, waiting for transfers between devices, shards(): lax.all_to_all(phase_image, 'acq', split_axis=1, concat_axis=0, tiled=True)  7.86 us
    all_to_all x1, starting transfers between devices, shards(): lax.all_to_all(slot_pixel[None], 'tile', split_axis=1, concat_axis=1, til...  7.28 us
    all_to_all x1, waiting for transfers between devices, shards(): lax.all_to_all(outgoing, 'tile', split_axis=1, concat_axis=1, tiled=True)  6.9 us
    all_to_all x1, waiting for transfers between devices, shards(): lax.all_to_all(sampled, 'tile', split_axis=1, concat_axis=1, tiled=True)  6.83 us
    gather x2, local copies, waits for them, and re-layouts, shards(): phases[:, send_list] - returned  6.35 us
  transfers between devices with their start and end apart: 8, of which 6 were waited for; matrix products, arithmetic and copies ran while one was open for 20% of the time, Pallas kernels for 0%

commit v1 on v0

--- a/solution.py
+++ b/solution.py
@@ -9,6 +9,29 @@
 RADIUS = 4
 SLAB_PIX = 8192
 min_weight = 0.1
+
+
+def split_up(x, dim, size):
+    shape = x.shape
+    parts = x.reshape(*shape[:dim], size, shape[dim] // size, *shape[dim + 1 :])
+    return jnp.moveaxis(parts, dim, 0)
+
+
+def joined_along(parts, dim):
+    parts = jnp.moveaxis(parts, 0, dim)
+    dims = parts.shape
+    return parts.reshape(*dims[:dim], dims[dim] * dims[dim + 1], *dims[dim + 2 :])
+
+
+def swapped_with_each(shard, axis, split_dim, concat_dim):
+    count, index = (lax.axis_size(axis), lax.axis_index(axis))
+    blocks = split_up(shard, split_dim, count)
+    outs = [blocks[index]]
+    for step in range(1, count):
+        sent = blocks[index ^ step]
+        outs.append(lax.ppermute(sent, axis, [(i, i ^ step) for i in range(count)]))
+    blocks = jnp.stack(outs)[index ^ jnp.arange(count)]
+    return joined_along(blocks, concat_dim)
 
 
 def with_halo(cells, sides, width):
@@ -84,9 +107,7 @@
     )
     weight_sum = jnp.zeros((SLAB_PIX,), jnp.float32).at[targets].add(arrived_weight.reshape(-1))
     series = lax.all_to_all(phase_image, "acq", split_axis=1, concat_axis=0, tiled=True)
-    phase_image = lax.all_to_all(
-        apply_highpass(highpass, series), "acq", split_axis=0, concat_axis=1, tiled=True
-    )
+    phase_image = swapped_with_each(apply_highpass(highpass, series), "acq", 0, 1)
     stacked = jnp.concatenate([phase_image, weight_sum[None, :]], axis=0).reshape(
         acq_loc + 1, ROWS_DEV, COLS
     )

time: 135 us -> 129 us (0.956)
  waiting for transfers between devices: 39.7 us -> 33.3 us
    ppermute x1, waiting for transfers between devices: 10.3 us -> 4.94 us  [with_halo(): lax.ppermute(tail, axis, [(i, (i + 1) % count) for i in range(ends)])]
    all_to_all x1 -> x0, starting transfers between devices: 3.47 us -> none  [shards(): lax.all_to_all(apply_highpass(highpass, series), 'acq', split_axis=0, con...]
    ppermute x1, waiting for transfers between devices: 0.01 us -> 3.06 us  [with_halo(): lax.ppermute(head, axis, [((i + 1) % count, i) for i in range(ends)])]
    all_to_all x1 -> x0, waiting for transfers between devices: 2.84 us -> none  [shards(): lax.all_to_all(apply_highpass(highpass, series), 'acq', split_axis=0, con...]
    ppermute x1, starting transfers between devices: 2.47 us -> 4.56 us  [with_halo(): lax.ppermute(tail, axis, [(i, (i + 1) % count) for i in range(ends)])]
    ppermute x0 -> x3, starting transfers between devices: none -> 1.92 us  [swapped_with_each(): outs.append(lax.ppermute(sent, axis, [(i, i ^ step) for i in range(count)]))]
  transfers between devices with their start and end apart: 8 -> 10, of which waited for: 6 -> 6; matrix products, arithmetic and copies ran while one was open for 20% -> 20% of each run, Pallas kernels for 0% -> 0%
where the time goes in v1:
time: 129 us; the launch traced here: 128 us
  local copies, waits for them, and re-layouts  41.5 us (32%)
  waiting for transfers between devices  33.3 us (26%)
  starting transfers between devices  32.7 us (25%)
  other arithmetic  19.4 us (15%)
    gather x1, local copies, waits for them, and re-layouts, shards(): slot_pixel = pixel_index[send_list]  10.5 us
    scatter-add x1, other arithmetic, shards(): jnp.zeros((acq_loc, SLAB_PIX), jnp.float32).at[:, targets]  8.2 us
    all_to_all x1, waiting for transfers between devices, shards(): lax.all_to_all(phase_image, 'acq', split_axis=1, concat_axis=0, tiled=True)  7.85 us
    all_to_all x1, starting transfers between devices, shards(): lax.all_to_all(slot_pixel[None], 'tile', split_axis=1, concat_axis=1, til...  7.28 us
    all_to_all x1, waiting for transfers between devices, shards(): lax.all_to_all(outgoing, 'tile', split_axis=1, concat_axis=1, tiled=True)  6.9 us
    all_to_all x1, waiting for transfers between devices, shards(): lax.all_to_all(sampled, 'tile', split_axis=1, concat_axis=1, tiled=True)  6.83 us
    gather x2, local copies, waits for them, and re-layouts, shards(): phases[:, send_list] - returned  6.36 us
    gather x1, local copies, waits for them, and re-layouts, shards(): slot_weight = jnp.where(live_slot, coherence[send_list], jnp.float32(0.0))  6.16 us
  transfers between devices with their start and end apart: 10, of which 6 were waited for; matrix products, arithmetic and copies ran while one was open for 20% of the time, Pallas kernels for 0%

profile of v1, /device:TPU:0, one launch (start us, length us, event | category | flops | bytes accessed | tf_op | source)
XLA Modules:
  0.0 128.4 jit_solution(2649015451825769976)
XLA Ops:
  0.6 0.0 copy-start
  0.6 0.0 copy-start.3
  0.7 0.8 fusion.58
  1.4 0.0 copy-done
  1.5 10.5 %gather_fusion.1 = s32[1024]{0:T(1024)} fusion(s32[16384]{0:T(1024)S(1)} %copy-done, s32[1024]{0:T(1024)S(1)} %fusion.58), kind=kCustom, calls=%fused_computation.1 | custom fusion | bytes 12288 | tf_op jit(solution)/shard_map/gather | solution.py:97
  12.0 7.3 %all-to-all-start = ((s32[1,8,128]{2,0,1:T(1,128)}), s32[1,8,128]{2,0,1:T(1,128)S(1)}, u32[]{:S(2)}, u32[]{:S(2)}) async-start(s32[1,8,128]{2,0,1:T(1,128)} %bitcast.5), calls=%async_computation | async-start | bytes 8192 | tf_op jit(solution)/shard_map/all_to_all | solution.py:102
  19.3 0.0 copy-done.3
  19.3 0.0 copy-start.1
  19.3 4.6 %copy.23 = f32[16,16384]{0,1:T(8,128)} copy(f32[16,16384]{1,0:T(8,128)S(1)} %copy-done.3) | data formatting | bytes 2097152 | tf_op args[0]
  23.9 0.0 copy-start.4
  23.9 6.2 %gather_fusion = f32[1024,16]{1,0:T(8,128)S(1)} fusion(f32[16,16384]{0,1:T(8,128)} %copy.23, s32[1024]{0:T(1024)S(1)} %fusion.58), kind=kCustom, calls=%fused_computation | custom fusion | bytes 135168 | tf_op jit(solution)/shard_map/gather | solution.py:120
  30.1 0.2 copy.24
  30.3 0.0 copy-done.1
  30.3 6.2 %gather_fusion.2 = f32[1024]{0:T(1024)S(1)} fusion(f32[16384]{0:T(1024)S(1)} %copy-done.1, s32[1024]{0:T(1024)S(1)} %fusion.58), kind=kCustom, calls=%fused_computation.2 | custom fusion | bytes 12288 | tf_op jit(solution)/shard_map/gather | solution.py:96
  36.5 0.0 copy-done.4
  36.5 0.1 bitcast_select_fusion
  36.6 0.6 bitcast_multiply_fusion
  37.2 0.0 all-to-all-done
  37.2 6.0 %all-to-all-start.1 = ((f32[16,8,128]{2,0,1:T(8,128)}), f32[16,8,128]{2,0,1:T(8,128)S(1)}, u32[]{:S(2)}, u32[]{:S(2)}) async-start(f32[16,8,128]{2,0,1:T(8,128)} %bitcast_multiply_fusion), calls=%async_computation.1 | async-start | bytes 131072 | tf_op jit(solution)/shard_map/all_to_all | solution.py:100
  43.2 6.9 %all-to-all-done.1 = f32[16,8,128]{2,0,1:T(8,128)S(1)} async-done(((f32[16,8,128]{2,0,1:T(8,128)}), f32[16,8,128]{2,0,1:T(8,128)S(1)}, u32[]{:S(2)}, u32[]{:S(2)}) %all-to-all-start.1) | async-done | bytes 65568 | tf_op jit(solution)/shard_map/all_to_all | solution.py:100
  50.1 0.2 copy.26
  50.3 0.0 copy-start.5
  50.3 8.2 %scatter_custom_fusion = f32[16,8192]{0,1:T(8,128)} fusion(s32[1024]{0:T(1024)S(1)} %bitcast.77, f32[1024,16]{1,0:T(8,128)S(1)} %copy.26, f32[]{:T(128)} %constant.22.clone.1), kind=kCustom, calls=%fused_computation.7 | custom fusion | flops 16384 | bytes 524292 | tf_op jit(solution)/shard_map/scatter-add | solution.py:106
  58.5 3.5 %copy.27 = f32[16,4,2048]{2,0,1:T(8,128)} copy(f32[16,4,2048]{0,2,1:T(8,128)} %bitcast.66) | data formatting | bytes 1048576 | tf_op jit(solution)/shard_map/all_to_all | solution.py:109
  62.0 3.5 %all-to-all-start.2 = ((f32[16,4,2048]{2,0,1:T(8,128)}), f32[16,4,2048]{2,0,1:T(8,128)S(1)}, u32[]{:S(2)}, u32[]{:S(2)}) async-start(f32[16,4,2048]{2,0,1:T(8,128)} %copy.27), calls=%async_computation.2 | async-start | bytes 1048576 | tf_op jit(solution)/shard_map/all_to_all | solution.py:109
  65.5 0.0 copy-done.5
  65.5 0.1 div.34
  65.6 0.1 le.27
  65.7 0.1 ge.32
  65.8 0.7 compare_select_fusion.1
  66.4 7.8 %all-to-all-done.2 = f32[16,4,2048]{2,0,1:T(8,128)S(1)} async-done(((f32[16,4,2048]{2,0,1:T(8,128)}), f32[16,4,2048]{2,0,1:T(8,128)S(1)}, u32[]{:S(2)}, u32[]{:S(2)}) %all-to-all-start.2) | async-done | bytes 524320 | tf_op jit(solution)/shard_map/all_to_all | solution.py:109
  74.3 3.3 %all-to-all-start.3 = ((f32[1,8,128]{2,0,1:T(1,128)}), f32[1,8,128]{2,0,1:T(1,128)S(1)}, u32[]{:S(2)}, u32[]{:S(2)}) async-start(f32[1,8,128]{2,0,1:T(1,128)} %compare_select_fusion.1), calls=%async_computation.3 | async-start | bytes 8192 | tf_op jit(solution)/shard_map/all_to_all | solution.py:101
  77.6 0.6 fusion.43
  78.3 0.1 collective-permute-start.2
  78.4 1.3 collective-permute-start.1
  79.6 0.6 collective-permute-start
  80.2 3.7 %all-to-all-done.3 = f32[1,8,128]{2,0,1:T(1,128)S(1)} async-done(((f32[1,8,128]{2,0,1:T(1,128)}), f32[1,8,128]{2,0,1:T(1,128)S(1)}, u32[]{:S(2)}, u32[]{:S(2)}) %all-to-all-start.3) | async-done | bytes 4128 | tf_op jit(solution)/shard_map/all_to_all | solution.py:101
  83.9 5.9 %scatter_custom_fusion.1 = f32[8192]{0:T(1024)S(1)} fusion(s32[1024]{0:T(1024)S(1)} %bitcast.78, f32[1024]{0:T(1024)S(1)} %bitcast.79, f32[]{:T(128)} %constant.22.clone.1), kind=kCustom, calls=%fused_computation.93 | custom fusion | flops 1024 | bytes 32772 | tf_op jit(solution)/shard_map/scatter-add | solution.py:108
  89.9 0.0 collective-permute-done.2
  89.9 0.0 collective-permute-done.1
  89.9 0.0 collective-permute-done
  90.0 0.6 gather_fusion.3
  90.6 0.3 copy.28
  90.9 0.2 concatenate.21
  91.2 0.1 fusion.62
  91.3 1.3 %collective-permute-start.4 = (f32[17,4,1024]{2,1,0:T(4,128)S(1)}, f32[17,4,1024]{2,1,0:T(4,128)S(1)}, u32[]{:S(2)}, u32[]{:S(2)}) collective-permute-start(f32[17,4,1024]{2,1,0:T(4,128)S(1)} %get-tuple-element.3), channel_id=1, source_target_pairs={{4,0},{8,4},{12,8},{16,12},{20,16},{24,20},{28,24},{5,1},{9,5},{13... | collective-permute-start | bytes 835592 | tf_op jit(solution)/shard_map/ppermute | solution.py:47
  92.6 4.6 %collective-permute-start.3 = (f32[17,4,1024]{2,1,0:T(4,128)S(1)}, f32[17,4,1024]{2,1,0:T(4,128)S(1)}, u32[]{:S(2)}, u32[]{:S(2)}) collective-permute-start(f32[17,4,1024]{2,1,0:T(4,128)S(1)} %get-tuple-element.2), channel_id=1, source_target_pairs={{0,4},{4,8},{8,12},{12,16},{16,20},{20,24},{24,28},{1,5},{5,9},{9,... | collective-permute-start | bytes 835592 | tf_op jit(solution)/shard_map/ppermute | solution.py:45
  97.2 3.1 %collective-permute-done.4 = f32[17,4,1024]{2,1,0:T(4,128)S(1)} collective-permute-done((f32[17,4,1024]{2,1,0:T(4,128)S(1)}, f32[17,4,1024]{2,1,0:T(4,128)S(1)}, u32[]{:S(2)}, u32[]{:S(2)}) %collective-permute-start.4) | collective-permute-done | bytes 278560 | tf_op jit(solution)/shard_map/ppermute | solution.py:47
  100.3 4.9 %collective-permute-done.3 = f32[17,4,1024]{2,1,0:T(4,128)S(1)} collective-permute-done((f32[17,4,1024]{2,1,0:T(4,128)S(1)}, f32[17,4,1024]{2,1,0:T(4,128)S(1)}, u32[]{:S(2)}, u32[]{:S(2)}) %collective-permute-start.3) | collective-permute-done | bytes 278560 | tf_op jit(solution)/shard_map/ppermute | solution.py:45
  105.2 1.0 fusion.21
  106.2 1.2 fusion.10
  107.5 0.1 slice_divide_fusion
  107.5 0.0 copy-start.2
  107.6 2.7 %copy.29 = f32[16,8,1024]{0,2,1:T(8,128)} copy(f32[16,8,1024]{2,1,0:T(8,128)S(1)} %slice_divide_fusion) | data formatting | bytes 1048576 | tf_op jit(solution)/shard_map/div | solution.py:116
  110.2 5.0 %gather_fusion.4 = f32[1024,16]{1,0:T(8,128)S(1)} fusion(f32[16,8192]{0,1:T(8,128)} %bitcast.67, s32[1024]{0:T(1024)S(1)} %fusion.60), kind=kCustom, calls=%fused_computation.4 | custom fusion | bytes 135168 | tf_op jit(solution)/shard_map/gather | solution.py:118
  115.2 0.8 copy.30
  116.0 4.8 %all-to-all-start.4 = ((f32[16,8,128]{2,0,1:T(8,128)}), f32[16,8,128]{2,0,1:T(8,128)S(1)}, u32[]{:S(2)}, u32[]{:S(2)}) async-start(f32[16,8,128]{2,0,1:T(8,128)} %bitcast.29), calls=%async_computation.4 | async-start | bytes 131072 | tf_op jit(solution)/shard_map/all_to_all | solution.py:119
  120.9 0.1 iota_compare_fusion.5
  121.0 6.8 %all-to-all-done.4 = f32[16,8,128]{2,0,1:T(8,128)S(1)} async-done(((f32[16,8,128]{2,0,1:T(8,128)}), f32[16,8,128]{2,0,1:T(8,128)S(1)}, u32[]{:S(2)}, u32[]{:S(2)}) %all-to-all-start.4) | async-done | bytes 65568 | tf_op jit(solution)/shard_map/all_to_all | solution.py:119
  127.8 0.6 copy_bitcast_fusion
  128.4 0.0 copy-done.2
  (13 shorter events, 0.2 us)
Async XLA Ops:
  0.6 0.8 copy-start
  0.6 18.7 %copy-start.3 = (f32[16,16384]{1,0:T(8,128)S(1)}, f32[16,16384]{1,0:T(8,128)}, u32[]{:S(2)}) copy-start(f32[16,16384]{1,0:T(8,128)} %param.6) | copy-start | bytes 3145732
  12.0 25.2 %all-to-all-start = ((s32[1,8,128]{2,0,1:T(1,128)}), s32[1,8,128]{2,0,1:T(1,128)S(1)}, u32[]{:S(2)}, u32[]{:S(2)}) async-start(s32[1,8,128]{2,0,1:T(1,128)} %bitcast.5), calls=%async_computation | async-start | bytes 8192 | tf_op jit(solution)/shard_map/all_to_all | solution.py:102
  19.3 11.0 %copy-start.1 = (f32[16384]{0:T(1024)S(1)}, f32[16384]{0:T(1024)}, u32[]{:S(2)}) copy-start(f32[16384]{0:T(1024)} %param.7) | copy-start | bytes 196612
  23.9 12.5 %copy-start.4 = (s32[1,8]{1,0:T(1,128)S(1)}, s32[1,8]{1,0:T(1,128)}, u32[]{:S(2)}) copy-start(s32[1,8]{1,0:T(1,128)} %param.10) | copy-start | bytes 100
  37.2 12.9 %all-to-all-start.1 = ((f32[16,8,128]{2,0,1:T(8,128)}), f32[16,8,128]{2,0,1:T(8,128)S(1)}, u32[]{:S(2)}, u32[]{:S(2)}) async-start(f32[16,8,128]{2,0,1:T(8,128)} %bitcast_multiply_fusion), calls=%async_computation.1 | async-start | bytes 131072 | tf_op jit(solution)/shard_map/all_to_all | solution.py:100
  50.3 15.2 %copy-start.5 = (s32[64]{0:T(128)S(1)}, s32[64]{0:T(128)}, u32[]{:S(2)}) copy-start(s32[64]{0:T(128)} %param.11) | copy-start | bytes 772
  62.0 12.3 %all-to-all-start.2 = ((f32[16,4,2048]{2,0,1:T(8,128)}), f32[16,4,2048]{2,0,1:T(8,128)S(1)}, u32[]{:S(2)}, u32[]{:S(2)}) async-start(f32[16,4,2048]{2,0,1:T(8,128)} %copy.27), calls=%async_computation.2 | async-start | bytes 1048576 | tf_op jit(solution)/shard_map/all_to_all | solution.py:109
  74.3 9.6 %all-to-all-start.3 = ((f32[1,8,128]{2,0,1:T(1,128)}), f32[1,8,128]{2,0,1:T(1,128)S(1)}, u32[]{:S(2)}, u32[]{:S(2)}) async-start(f32[1,8,128]{2,0,1:T(1,128)} %compare_select_fusion.1), calls=%async_computation.3 | async-start | bytes 8192 | tf_op jit(solution)/shard_map/all_to_all | solution.py:101
  78.3 11.6 %collective-permute-start.2 = (f32[16,2048]{1,0:T(8,128)S(1)}, f32[16,2048]{1,0:T(8,128)S(1)}, u32[]{:S(2)}, u32[]{:S(2)}) collective-permute-start(f32[16,2048]{1,0:T(8,128)S(1)} %get-tuple-element.5), channel_id=1, source_target_pairs={{0,3},{1,2},{2,1},{3,0},{4,7},{5,6},{6,5},{7,4},{8,11},{9,10},{10,... | collective-permute-start | bytes 393224 | tf_op jit(solution)/shard_map/ppermute | solution.py:32
  78.4 11.5 %collective-permute-start.1 = (f32[16,2048]{1,0:T(8,128)S(1)}, f32[16,2048]{1,0:T(8,128)S(1)}, u32[]{:S(2)}, u32[]{:S(2)}) collective-permute-start(f32[16,2048]{1,0:T(8,128)S(1)} %get-tuple-element.6), channel_id=1, source_target_pairs={{0,2},{1,3},{2,0},{3,1},{4,6},{5,7},{6,4},{7,5},{8,10},{9,11},{10,... | collective-permute-start | bytes 393224 | tf_op jit(solution)/shard_map/ppermute | solution.py:32
  79.6 10.3 %collective-permute-start = (f32[16,2048]{1,0:T(8,128)S(1)}, f32[16,2048]{1,0:T(8,128)S(1)}, u32[]{:S(2)}, u32[]{:S(2)}) collective-permute-start(f32[16,2048]{1,0:T(8,128)S(1)} %get-tuple-element.7), channel_id=1, source_target_pairs={{0,1},{1,0},{2,3},{3,2},{4,5},{5,4},{6,7},{7,6},{8,9},{9,8},{10,11... | collective-permute-start | bytes 393224 | tf_op jit(solution)/shard_map/ppermute | solution.py:32
  91.3 8.9 %collective-permute-start.4 = (f32[17,4,1024]{2,1,0:T(4,128)S(1)}, f32[17,4,1024]{2,1,0:T(4,128)S(1)}, u32[]{:S(2)}, u32[]{:S(2)}) collective-permute-start(f32[17,4,1024]{2,1,0:T(4,128)S(1)} %get-tuple-element.3), channel_id=1, source_target_pairs={{4,0},{8,4},{12,8},{16,12},{20,16},{24,20},{28,24},{5,1},{9,5},{13... | collective-permute-start | bytes 835592 | tf_op jit(solution)/shard_map/ppermute | solution.py:47
  92.6 12.6 %collective-permute-start.3 = (f32[17,4,1024]{2,1,0:T(4,128)S(1)}, f32[17,4,1024]{2,1,0:T(4,128)S(1)}, u32[]{:S(2)}, u32[]{:S(2)}) collective-permute-start(f32[17,4,1024]{2,1,0:T(4,128)S(1)} %get-tuple-element.2), channel_id=1, source_target_pairs={{0,4},{4,8},{8,12},{12,16},{16,20},{20,24},{24,28},{1,5},{5,9},{9,... | collective-permute-start | bytes 835592 | tf_op jit(solution)/shard_map/ppermute | solution.py:45
  107.5 20.9 %copy-start.2 = (f32[16,8,1024]{2,1,0:T(8,128)}, f32[16,8,1024]{2,1,0:T(8,128)S(1)}, u32[]{:S(2)}) copy-start(f32[16,8,1024]{2,1,0:T(8,128)S(1)} %slice_divide_fusion) | copy-start | bytes 1572868
  116.0 11.8 %all-to-all-start.4 = ((f32[16,8,128]{2,0,1:T(8,128)}), f32[16,8,128]{2,0,1:T(8,128)S(1)}, u32[]{:S(2)}, u32[]{:S(2)}) async-start(f32[16,8,128]{2,0,1:T(8,128)} %bitcast.29), calls=%async_computation.4 | async-start | bytes 131072 | tf_op jit(solution)/shard_map/all_to_all | solution.py:119
